TPU v7x, 32 devices: a whole 2x2x4 slice. The times are simulated.
32 devices in a mesh: expert: 4 (over z), dp: 8 (over y, x, core).
Axes of the slice: x: 2, y: 2, z: 4, core: 2. Of those that a mesh axis runs over, the one named last changes fastest.
Arguments:
- tokens: bfloat16 [1024, 1408], P('dp', 'expert'), may hold values from -6 to 6
- routes: int32 [1024, 2], P('dp'), may hold values from 0 to 7, all different within a row; in each aligned block of 128 rows (0 to 127, 128 to 255, ...) at most 40 rows name the same one
- gate_values: float32 [1024, 2], P('dp'), may hold values from 0.2 to 1
- expert_in: bfloat16 [8, 1408, 6144], P('expert', None, 'dp'), may hold values from -0.15625 to 0.15625
- expert_out: bfloat16 [8, 6144, 1408], P('expert', 'dp'), may hold values from -0.078125 to 0.078125
- cotangent: bfloat16 [1024, 1408], P('dp', 'expert'), may hold values from -1.1953125 to 1.1953125
Outputs:
- layer_out: bfloat16 [1024, 1408], P('dp', 'expert')
- grad_tokens: bfloat16 [1024, 1408], P('dp', 'expert')
- grad_gates: float32 [1024, 2], P('dp')
- grad_in: bfloat16 [8, 1408, 6144], P('expert', None, 'dp')
- grad_out: bfloat16 [8, 6144, 1408], P('expert', 'dp')
Inputs may be any that keep to these rules, and one draw needn't show every extreme that they name: `routes`: each row names two different experts. In each aligned block of 128 rows no expert is named by more than 40 rows, a bound that some block reaches.
All inputs are finite; a program needn't handle non-finite values.
Results may differ from a plain program's by a relative error of at most 0.014.
Values may be sent and summed in bfloat16 or wider, within the bound.
A program may use at most 128 MiB of HBM per device.

v0:
```python
import jax
import jax.numpy as jnp
from jax import lax
from jax.sharding import PartitionSpec as P


def gelu_tanh(values):
    return jax.nn.gelu(values, approximate=True)


def shards(tokens, routes, gate_values, expert_in, expert_out, cotangent):
    tok_dev, columns = tokens.shape
    groups = lax.axis_size("expert")
    per_dev = expert_in.shape[0]
    experts = per_dev * groups
    capacity = 5 * tok_dev // (2 * experts)
    full_width = columns * groups
    slot_rows = per_dev * capacity
    slot_count = experts * capacity
    flat_routes = routes.reshape(-1)
    onehot = (flat_routes[:, None] == jnp.arange(experts, dtype=jnp.int32)[None, :]).astype(
        jnp.int32
    )
    rank_in = jnp.sum((jnp.cumsum(onehot, axis=0, dtype=jnp.int32) - onehot) * onehot, axis=1)
    owner_idx = flat_routes // per_dev
    within = flat_routes % per_dev
    slot_ids = (within * capacity + rank_in) * groups + owner_idx
    placing = (slot_ids[:, None] == jnp.arange(slot_count, dtype=jnp.int32)[None, :]).astype(
        jnp.bfloat16
    )
    pair_gates = gate_values.reshape(-1)
    pair_tokens = jnp.repeat(tokens, 2, axis=0)
    cot_float = cotangent.astype(jnp.float32)
    pair_cot = (jnp.repeat(cot_float, 2, axis=0) * pair_gates[:, None]).astype(jnp.bfloat16)

    def to_slots(pairs):
        slots = jnp.einsum("ps,pc->sc", placing, pairs, preferred_element_type=jnp.float32)
        return slots.astype(jnp.bfloat16).reshape(slot_rows, groups, columns)

    def from_slots(back):
        return jnp.einsum(
            "ps,sc->pc",
            placing,
            back.reshape(slot_count, columns),
            preferred_element_type=jnp.float32,
        )

    def as_rows(gathered):
        return gathered.reshape(-1, per_dev, capacity, full_width)

    x_moved = lax.all_to_all(
        to_slots(pair_tokens), "expert", split_axis=1, concat_axis=1, tiled=True
    )
    x_rows = as_rows(
        lax.all_gather(x_moved.reshape(slot_rows, full_width), "dp", axis=0, tiled=True)
    )
    pre_act = jnp.einsum("bjcd,jdf->bjcf", x_rows, expert_in, preferred_element_type=jnp.float32)
    pre_act, hidden = (pre_act, gelu_tanh(pre_act).astype(jnp.bfloat16))
    part = hidden
    term = jnp.einsum("bjcf,jfd->bjcd", part, expert_out, preferred_element_type=jnp.float32)
    out_sum = lax.psum_scatter(
        term.reshape(lax.axis_size("dp") * slot_rows, full_width).astype(jnp.bfloat16),
        "dp",
        scatter_dimension=0,
        tiled=True,
    )
    out_back = lax.all_to_all(
        out_sum.reshape(slot_rows, groups, columns),
        "expert",
        split_axis=1,
        concat_axis=1,
        tiled=True,
    )
    dy_moved = lax.all_to_all(to_slots(pair_cot), "expert", split_axis=1, concat_axis=1, tiled=True)
    dy_rows = as_rows(
        lax.all_gather(dy_moved.reshape(slot_rows, full_width), "dp", axis=0, tiled=True)
    )
    d_hidden = jnp.einsum("bjcd,jfd->bjcf", dy_rows, expert_out, preferred_element_type=jnp.float32)
    backward_d_pre = jax.vjp(gelu_tanh, pre_act)[1](d_hidden)[0].astype(jnp.bfloat16)
    grad_out = jnp.einsum("bjcf,bjcd->jfd", hidden, dy_rows, preferred_element_type=jnp.float32)
    grad_in = jnp.einsum(
        "bjcd,bjcf->jdf", x_rows, backward_d_pre, preferred_element_type=jnp.float32
    )
    d_pre, grad_in, grad_out = (
        backward_d_pre,
        grad_in.astype(jnp.bfloat16),
        grad_out.astype(jnp.bfloat16),
    )
    part = d_pre
    term = jnp.einsum("bjcf,jdf->bjcd", part, expert_in, preferred_element_type=jnp.float32)
    dx_sum = lax.psum_scatter(
        term.reshape(lax.axis_size("dp") * slot_rows, full_width).astype(jnp.bfloat16),
        "dp",
        scatter_dimension=0,
        tiled=True,
    )
    dx_back = lax.all_to_all(
        dx_sum.reshape(slot_rows, groups, columns),
        "expert",
        split_axis=1,
        concat_axis=1,
        tiled=True,
    )
    out_view = from_slots(out_back).reshape(tok_dev, 2, columns)
    dx_view = from_slots(dx_back).reshape(tok_dev, 2, columns)
    gate_pairs = pair_gates.reshape(tok_dev, 2)
    layer_out = (out_view[:, 0] * gate_pairs[:, 0:1] + out_view[:, 1] * gate_pairs[:, 1:2]).astype(
        jnp.bfloat16
    )
    grad_tokens = (dx_view[:, 0] + dx_view[:, 1]).astype(jnp.bfloat16)
    gate_part = jnp.sum(cot_float[:, None, :] * out_view, axis=2)
    grad_gates = lax.psum(gate_part, "expert")
    return (layer_out, grad_tokens, grad_gates, grad_in, grad_out)


def solution(mesh):
    placed = (
        P("dp", "expert"),
        P("dp", None),
        P("dp", None),
        P("expert", None, "dp"),
        P("expert", "dp", None),
        P("dp", "expert"),
    )
    return jax.shard_map(
        shards,
        mesh=mesh,
        in_specs=placed,
        out_specs=(
            P("dp", "expert"),
            P("dp", "expert"),
            P("dp", None),
            P("expert", None, "dp"),
            P("expert", "dp", None),
        ),
        check_vma=False,
    )
```

profile of v0, /device:TPU:0, one launch (start us, length us, event | category | flops | bytes accessed | tf_op | source)
XLA Modules:
  0.0 206.7 jit_solution(3152823951427038847)
XLA Ops:
  7.2 0.8 copy.58
  8.0 0.1 eq.71
  8.1 0.1 eq.67
  8.3 0.6 reduce-window.6
  8.9 0.2 slice_reduce_fusion
  9.3 1.0 copy.61
  10.3 0.1 broadcast_in_dim.4
  10.4 0.2 reshape.167
  10.6 0.4 convolution_convert_fusion.1
  11.1 14.7 %all_to_all.20 = bf16[80,4,352]{2,0,1:T(8,128)(2,1)S(1)} all-to-all(bf16[80,4,352]{2,0,1:T(8,128)(2,1)S(1)} %copy.62), channel_id=1, replica_groups=mesh['expert'=4,'dp'=8] {'expert'}, dimensions={1} | all-to-all | bytes 450560 | tf_op jit(solution)/shard_map/all_to_all | solution.py:51
  25.9 0.9 reshape.169
  26.8 0.1 copy.81
  26.9 0.1 broadcast_in_dim.5.clone
  27.1 0.3 reshape.173
  27.4 0.1 copy.69
  27.5 0.1 mul.135
  27.6 0.4 convolution_convert_fusion
  28.1 10.7 %all_to_all.21 = bf16[80,4,352]{2,0,1:T(8,128)(2,1)S(1)} all-to-all(bf16[80,4,352]{2,0,1:T(8,128)(2,1)S(1)} %copy.70), channel_id=1, replica_groups=mesh['expert'=4,'dp'=8] {'expert'}, dimensions={1} | all-to-all | bytes 450560 | tf_op jit(solution)/shard_map/all_to_all | solution.py:74
  38.9 0.9 reshape.175
  39.9 12.7 %all-gather.3.cloned.1.call-done = bf16[640,1408]{1,0:T(8,128)(2,1)} async-done(((bf16[80,1408]{1,0:T(8,128)(2,1)}), bf16[640,1408]{1,0:T(8,128)(2,1)}) %all-gather.3.cloned.1.call-update) | async-done | bytes 1802256 | tf_op jit(solution)/shard_map/all_gather | solution.py:55
  52.6 4.5 %fusion.2 = f32[2,8,40,768]{3,2,1,0:T(8,128)S(1)} fusion(bf16[2,1408,768]{2,1,0:T(8,128)(2,1)} %param.9, bf16[8,2,40,1408]{3,2,1,0:T(8,128)(2,1)} %bitcast.106), kind=kOutput, calls=%fused_computation.4 | convolution fusion | flops 1384120320 | bytes 8093696 | tf_op jit(solution)/shard_map/bjcd,jdf->bjcf/dot_general | solution.py:57
  57.1 24.0 %all-gather.5.cloned.1.call-done = bf16[640,1408]{1,0:T(8,128)(2,1)} async-done(((bf16[80,1408]{1,0:T(8,128)(2,1)}), bf16[640,1408]{1,0:T(8,128)(2,1)}) %all-gather.5.cloned.1.call-update) | async-done | bytes 1802256 | tf_op jit(solution)/shard_map/all_gather | solution.py:76
  81.0 5.4 %fusion.26 = bf16[8,2,40,768]{3,2,0,1:T(8,128)(2,1)S(1)} fusion(f32[2,8,40,768]{3,2,1,0:T(8,128)S(1)} %fusion.2, bf16[2,768,1408]{2,1,0:T(8,128)(2,1)} %param.10, bf16[8,2,40,1408]{3,2,1,0:T(8,128)(2,1)} %bitcast.108), kind=kOutput, calls=%fused_computation.22 | convolution fusion | flops 1393950720 | bytes 9076736 | tf_op jit(solution)/shard_map/bjcd,jfd->bjcf/dot_general | solution.py:78
  86.4 4.0 %fusion.14 = bf16[8,2,40,1408]{3,2,0,1:T(8,128)(2,1)S(1)} fusion(bf16[8,2,40,768]{3,2,0,1:T(8,128)(2,1)S(1)} %fusion.26, bf16[2,1408,768]{2,1,0:T(8,128)(2,1)} %param.9), kind=kOutput, calls=%fused_computation.12 | convolution fusion | flops 1385021440 | bytes 7110656 | tf_op jit(solution)/shard_map/bjcf,jdf->bjcd/dot_general | solution.py:90
  90.4 1.4 copy.73
  91.8 0.2 reduce-scatter.3.cloned.1.call-start
  92.1 4.0 %fusion.17 = bf16[8,2,40,1408]{3,2,0,1:T(8,128)(2,1)S(1)} fusion(bf16[2,768,1408]{2,1,0:T(8,128)(2,1)} %param.10, f32[2,8,40,768]{3,2,1,0:T(8,128)S(1)} %fusion.2), kind=kOutput, calls=%fused_computation.13 | convolution fusion | flops 1389445120 | bytes 8093696 | tf_op jit(solution)/shard_map/bjcf,jfd->bjcd/dot_general | solution.py:60
  96.1 1.4 copy.65
  97.5 0.1 reduce_sum.21
  97.7 0.4 copy-done.1
  98.2 7.2 %bitcast_convert_fusion = bf16[2,768,1408]{2,1,0:T(8,128)(2,1)} fusion(bf16[8,2,40,1408]{3,2,1,0:T(8,128)(2,1)} %bitcast.109, f32[2,8,40,768]{3,2,1,0:T(8,128)} %copy-done.4), kind=kOutput, calls=%fused_computation | convolution fusion | flops 1390706688 | bytes 8093696 | tf_op jit(solution)/shard_map/bjcf,bjcd->jfd/dot_general | solution.py:80
  105.3 25.8 %reduce-scatter.5.cloned.1.call-done = bf16[80,1408]{1,0:T(8,128)(2,1)} async-done(((bf16[640,1408]{1,0:T(8,128)(2,1)}), bf16[80,1408]{1,0:T(8,128)(2,1)}) %reduce-scatter.5.cloned.1.call-update) | async-done | bytes 225296 | tf_op jit(solution)/shard_map/reduce_scatter | solution.py:91
  131.1 1.2 reshape.177
  132.3 0.7 copy.74
  133.1 4.6 %all-to-all-start.3 = ((bf16[80,4,352]{2,0,1:T(8,128)(2,1)}), bf16[80,4,352]{2,0,1:T(8,128)(2,1)S(1)}, u32[]{:S(2)}, u32[]{:S(2)}) async-start(bf16[80,4,352]{2,0,1:T(8,128)(2,1)} %copy.74), calls=%async_computation.5 | async-start | bytes 491520 | tf_op jit(solution)/shard_map/all_to_all | solution.py:97
  137.7 4.5 %bitcast_convert_fusion.1 = bf16[2,1408,768]{2,1,0:T(8,128)(2,1)} fusion(bf16[8,2,40,1408]{3,2,1,0:T(8,128)(2,1)S(1)} %bitcast.107, bf16[8,2,40,768]{3,2,0,1:T(8,128)(2,1)S(1)} %fusion.26), kind=kOutput, calls=%fused_computation.1 | convolution fusion | flops 1386283008 | bytes 7110656 | tf_op jit(solution)/shard_map/bjcd,bjcf->jdf/dot_general | solution.py:81
  142.2 31.5 %reduce-scatter.3.cloned.1.call-done = bf16[80,1408]{1,0:T(8,128)(2,1)} async-done(((bf16[640,1408]{1,0:T(8,128)(2,1)}), bf16[80,1408]{1,0:T(8,128)(2,1)}) %reduce-scatter.3.cloned.1.call-update) | async-done | bytes 225296 | tf_op jit(solution)/shard_map/reduce_scatter | solution.py:61
  173.7 1.2 reshape.171
  174.9 0.7 copy.66
  175.6 4.6 %all-to-all-start.1 = ((bf16[80,4,352]{2,0,1:T(8,128)(2,1)}), bf16[80,4,352]{2,0,1:T(8,128)(2,1)S(1)}, u32[]{:S(2)}, u32[]{:S(2)}) async-start(bf16[80,4,352]{2,0,1:T(8,128)(2,1)} %copy.66), calls=%async_computation.2 | async-start | bytes 491520 | tf_op jit(solution)/shard_map/all_to_all | solution.py:67
  180.3 0.1 reshape.182
  180.5 0.3 fusion.40
  180.8 0.7 fusion.54
  181.4 7.2 %all-to-all-done.1 = bf16[80,4,352]{2,0,1:T(8,128)(2,1)S(1)} async-done(((bf16[80,4,352]{2,0,1:T(8,128)(2,1)}), bf16[80,4,352]{2,0,1:T(8,128)(2,1)S(1)}, u32[]{:S(2)}, u32[]{:S(2)}) %all-to-all-start.1) | async-done | bytes 225312 | tf_op jit(solution)/shard_map/all_to_all | solution.py:67
  188.7 0.1 reshape.181
  188.8 0.3 multiply_reduce_fusion
  189.1 10.4 %psum.7 = f32[128,2]{0,1:T(2,128)} all-reduce(f32[128,2]{0,1:T(2,128)S(1)} %get-tuple-element.7), channel_id=1, replica_groups=mesh['expert'=4,'dp'=8] {'expert'}, use_global_device_ids=true, to_apply=%region_6.7 | all-reduce | flops 256 | bytes 2048 | tf_op jit(solution)/shard_map/psum | solution.py:112
  199.5 0.7 fusion.50
  (34 shorter events, 1.0 us)
Async XLA Ops:
  7.2 45.4 %all-gather.3.cloned.1.call-start = ((), (), s32[]{:S(2)}) async-start(), calls=%async_computation.6 | async-start | bytes 2027520 | tf_op jit(solution)/shard_map/all_gather | solution.py:55
  9.2 17.6 %copy-start = (bf16[128,352]{0,1:T(8,128)(2,1)S(1)}, bf16[128,352]{0,1:T(8,128)(2,1)}, u32[]{:S(2)}) copy-start(bf16[128,352]{0,1:T(8,128)(2,1)} %param.11) | copy-start | bytes 270340
  11.0 16.3 %copy-start.2 = (f32[128,2]{0,1:T(2,128)S(1)}, f32[128,2]{0,1:T(2,128)}, u32[]{:S(2)}) copy-start(f32[128,2]{0,1:T(2,128)} %param.8) | copy-start | bytes 3076
  26.8 54.2 %all-gather.5.cloned.1.call-start = ((), (), s32[]{:S(2)}) async-start(), calls=%async_computation.8 | async-start | bytes 2027520 | tf_op jit(solution)/shard_map/all_gather | solution.py:76
  39.8 91.3 %reduce-scatter.5.cloned.1.call-start = ((), (), s32[]{:S(2)}) async-start(), calls=%async_computation.9 | async-start | bytes 2027520 | tf_op jit(solution)/shard_map/reduce_scatter | solution.py:91
  57.0 35.0 %copy-start.4 = (f32[2,8,40,768]{3,2,1,0:T(8,128)}, f32[2,8,40,768]{3,2,1,0:T(8,128)S(1)}, u32[]{:S(2)}) copy-start(f32[2,8,40,768]{3,2,1,0:T(8,128)S(1)} %fusion.2) | copy-start | bytes 5898244
  91.8 81.9 %reduce-scatter.3.cloned.1.call-start = ((), (), s32[]{:S(2)}) async-start(), calls=%async_computation.7 | async-start | bytes 2027520 | tf_op jit(solution)/shard_map/reduce_scatter | solution.py:61
  97.5 0.7 copy-start.1
  98.2 39.5 %copy-start.3 = (bf16[640,1408]{1,0:T(8,128)(2,1)S(1)}, bf16[640,1408]{1,0:T(8,128)(2,1)}, u32[]{:S(2)}) copy-start(bf16[640,1408]{1,0:T(8,128)(2,1)} %all-gather.3.cloned.1.call-done) | copy-start | bytes 5406724
  133.1 42.6 %all-to-all-start.3 = ((bf16[80,4,352]{2,0,1:T(8,128)(2,1)}), bf16[80,4,352]{2,0,1:T(8,128)(2,1)S(1)}, u32[]{:S(2)}, u32[]{:S(2)}) async-start(bf16[80,4,352]{2,0,1:T(8,128)(2,1)} %copy.74), calls=%async_computation.5 | async-start | bytes 491520 | tf_op jit(solution)/shard_map/all_to_all | solution.py:97
  175.6 13.0 %all-to-all-start.1 = ((bf16[80,4,352]{2,0,1:T(8,128)(2,1)}), bf16[80,4,352]{2,0,1:T(8,128)(2,1)S(1)}, u32[]{:S(2)}, u32[]{:S(2)}) async-start(bf16[80,4,352]{2,0,1:T(8,128)(2,1)} %copy.66), calls=%async_computation.2 | async-start | bytes 491520 | tf_op jit(solution)/shard_map/all_to_all | solution.py:67
Sparse Core Ops, SparseCore 0:
  26.9 25.6 all-gather.2
  54.5 26.5 all-gather.4
  91.9 39.1 reduce-scatter.4
  134.5 39.1 reduce-scatter.2
where the time goes:
time: 207 us
  waiting for transfers between devices  101 us (49%)
  blocking collectives  35.7 us (17%)
  matrix products  30.9 us (15%)
  between operations  14 us (7%)
  local copies, waits for them, and re-layouts  13.2 us (6%)
  starting transfers between devices  9.54 us (5%)
  other arithmetic  2.09 us (1%)
    reduce_scatter x2, waiting for transfers between devices, shards(): lax.psum_scatter(term.reshape(lax.axis_size('dp') * slot_rows, full_width...  57.4 us
    all_gather x1, waiting for transfers between devices, shards(): lax.all_gather(dy_moved.reshape(slot_rows, full_width), 'dp', axis=0, til...  24 us
    all_to_all x1, blocking collectives, shards(): lax.all_to_all(to_slots(pair_tokens), 'expert', split_axis=1, concat_axis...  14.7 us
    all_gather x1, waiting for transfers between devices, shards(): lax.all_gather(x_moved.reshape(slot_rows, full_width), 'dp', axis=0, tile...  12.7 us
    all_to_all x1, blocking collectives, shards(): lax.all_to_all(to_slots(pair_cot), 'expert', split_axis=1, concat_axis=1,...  10.7 us
    psum x1, blocking collectives, shards(): grad_gates = lax.psum(gate_part, 'expert')  10.4 us
    dot_general x1, matrix products, shards(): jnp.einsum('bjcf,bjcd->jfd', hidden, dy_rows, preferred_element_type=jnp....  7.18 us
    all_to_all x1, waiting for transfers between devices, shards(): lax.all_to_all(out_sum.reshape(slot_rows, groups, columns), 'expert', spl...  7.17 us
  transfers between devices with their start and end apart: 6, of which 5 were waited for; matrix products, arithmetic and copies ran while one was open for 14% of the time, Pallas kernels for 0%

commit v1 on v0

--- a/solution.py
+++ b/solution.py
@@ -1,6 +1,8 @@
 import jax
 import jax.numpy as jnp
 from jax import lax
+from jax.experimental import pallas as pl
+from jax.experimental.pallas import tpu as pltpu
 from jax.sharding import PartitionSpec as P
 
 
@@ -113,6 +115,375 @@
     return (layer_out, grad_tokens, grad_gates, grad_in, grad_out)
 
 
+MESH = pl.DeviceIdType.MESH
+BF16 = jnp.bfloat16
+F32 = jnp.float32
+
+
+def tiles_of(width, step=256):
+    return [(lo, min(step, width - lo)) for lo in range(0, width, step)]
+
+
+def dot(left, right, contract):
+    return lax.dot_general(left, right, ((contract[:1], contract[1:]), ((), ())), preferred_element_type=F32)
+
+
+def layer_kernel(
+    tok_ref, cot_ref, routes_t, gates_t, gates_ref, w_in_hbm, w_out_hbm,
+    out_ref, gtok_ref, gg_ref, gi_hbm, go_hbm,
+    w_in, w_out, gi, go, slots, zgot, gath, rows, hid, slope, dpre,
+    term, mate, sums, relay, landed, zsend, zback, place, gpart,
+    wsem, osem, a2a_s, a2a_r, ag_s, ag_r, mate_s, mate_r, rs_s, rs_r, back_s, back_r, gg_s, gg_r,
+):
+    tok_dev, cols = tok_ref.shape
+    zs = slots.shape[1]
+    per_rows = slots.shape[2]
+    per_dev = w_in.shape[0]
+    cap = per_rows // per_dev
+    width, hidden_here = w_in.shape[1:]
+    experts = zs * per_dev
+    z = lax.axis_index("expert")
+    d = lax.axis_index("dp")
+    core = d % 2
+    xbit = (d // 2) % 2
+    ybit = d // 4
+    mate_d = d + 1 - 2 * core
+    xn = d + 2 - 4 * xbit
+    yn = d + 4 - 8 * ybit
+    dd = xn + 4 - 8 * ybit
+    first = core * yn + (1 - core) * xn
+    second = core * xn + (1 - core) * yn
+
+    def remote(src, dst, send, recv, zi, di):
+        return pltpu.make_async_remote_copy(
+            src_ref=src, dst_ref=dst, send_sem=send, recv_sem=recv, device_id=(zi, di), device_id_type=MESH
+        )
+
+    barrier = pltpu.get_barrier_semaphore()
+    for step in range(1, zs):
+        pl.semaphore_signal(barrier, inc=1, device_id=((z + step) % zs, d), device_id_type=MESH)
+    for other in (mate_d, xn, yn):
+        pl.semaphore_signal(barrier, inc=1, device_id=(z, other), device_id_type=MESH)
+
+    w_copies = []
+    for j in range(per_dev):
+        w_copies.append(pltpu.make_async_copy(w_in_hbm.at[j], w_in.at[j], wsem.at[0, j]))
+        w_copies.append(pltpu.make_async_copy(w_out_hbm.at[j], w_out.at[j], wsem.at[1, j]))
+    for copy in w_copies:
+        copy.start()
+
+    named = lax.broadcasted_iota(jnp.int32, (experts, tok_dev), 0)
+    first_of = (named == routes_t[0:1, :]).astype(F32)
+    second_of = (named == routes_t[1:2, :]).astype(F32)
+    before = (
+        lax.broadcasted_iota(jnp.int32, (tok_dev, tok_dev), 0)
+        < lax.broadcasted_iota(jnp.int32, (tok_dev, tok_dev), 1)
+    ).astype(F32).astype(BF16)
+    earlier = dot((first_of + second_of).astype(BF16), before, (1, 0))
+    slot_iota = lax.broadcasted_iota(jnp.int32, (experts * cap, tok_dev), 0)
+    gate_col = jnp.zeros((experts * cap, 1), F32)
+    for k, of in ((0, first_of), (1, second_of)):
+        rank = jnp.sum(earlier * of, axis=0, keepdims=True).astype(jnp.int32)
+        taken = (slot_iota == routes_t[k : k + 1, :] * cap + rank).astype(F32)
+        place[k] = taken.astype(BF16)
+        gate_col = gate_col + jnp.sum(taken * gates_t[k : k + 1, :], axis=1, keepdims=True)
+    both = place[0] + place[1]
+    slots[0] = dot(both, tok_ref[...], (1, 0)).astype(BF16).reshape(zs, per_rows, cols)
+    slots[1] = (dot(both, cot_ref[...], (1, 0)) * gate_col).astype(BF16).reshape(zs, per_rows, cols)
+    for a in range(2):
+        zgot[a, pl.ds(z, 1)] = slots[a, pl.ds(z, 1)]
+
+    pl.semaphore_wait(barrier, zs + 2)
+
+    a2a = []
+    for a in range(2):
+        a2a.append([])
+        for step in range(1, zs):
+            to = (z + step) % zs
+            copy = remote(
+                slots.at[a, to], zgot.at[a, z], a2a_s.at[a, step - 1], a2a_r.at[a, step - 1], to, d
+            )
+            copy.start()
+            a2a[a].append(copy)
+
+    def ag_copy(a, i):
+        block, to = (
+            (d, xn), (d, yn), (d, mate_d),
+            (second, first), (xn, mate_d), (yn, mate_d), (dd, mate_d),
+        )[i]
+        return remote(gath.at[a, block], gath.at[a, block], ag_s.at[a, i], ag_r.at[a, i], z, to)
+
+    ag = [[ag_copy(a, i) for i in range(7)] for a in range(2)]
+
+    def assemble(a):
+        for copy in a2a[a]:
+            copy.wait()
+        whole = jnp.concatenate([zgot[a, i].astype(F32) for i in range(zs)], axis=-1)
+        gath[a, pl.ds(d, 1)] = whole.astype(BF16)[None]
+        for i in range(3):
+            ag[a][i].start()
+
+    def forward(a):
+        ag[a][0].wait_recv()
+        ag[a][1].wait_recv()
+        for i in (3, 4, 5):
+            ag[a][i].start()
+
+    def forward_last(a):
+        ag[a][3].wait_recv()
+        ag[a][6].start()
+
+    def finish(a):
+        for i in (2, 4, 5, 6):
+            ag[a][i].wait_recv()
+
+        def column(n, carry):
+            at = pl.ds(pl.multiple_of(n * 128, 128), 128)
+            for half in range(2):
+                blocks = [gath[a, 2 * chip + half, :, at].astype(F32) for chip in range(4)]
+                for w in range(per_dev):
+                    picked = jnp.concatenate([b[w * cap : (w + 1) * cap] for b in blocks], axis=0)
+                    rows[a, w, half * 4 * cap : (half + 1) * 4 * cap, at] = picked.astype(BF16)
+            return carry
+
+        lax.fori_loop(0, width // 128, column, 0)
+
+    def activation(j):
+        def column(n, carry):
+            at = pl.ds(pl.multiple_of(n * 256, 256), 256)
+            v = dot(rows[0, j], w_in[j, :, at], (1, 0))
+            scale = 0.7978845608028654
+            sq = v * v
+            t = jnp.tanh(scale * v * (1.0 + 0.044715 * sq))
+            half = 0.5 * (1.0 + t)
+            hid[j, :, at] = (v * half).astype(BF16)
+            slope[j, :, at] = half + 0.5 * v * (1.0 - t * t) * (scale * (1.0 + 0.134145 * sq))
+            return carry
+
+        lax.fori_loop(0, hidden_here // 256, column, 0)
+
+    def backward(j):
+        def column(n, carry):
+            at = pl.ds(pl.multiple_of(n * 256, 256), 256)
+            dh = dot(rows[1, j], w_out[j, at, :], (1, 1))
+            dpre[j, :, at] = (slope[j, :, at] * dh).astype(BF16)
+            return carry
+
+        lax.fori_loop(0, hidden_here // 256, column, 0)
+
+    half_rows = 4 * cap
+
+    def mate_copy(a, j):
+        return remote(
+            term.at[a, j, 1 - core], mate.at[a, j], mate_s.at[a, j], mate_r.at[a, j], z, mate_d
+        )
+
+    mates = [[mate_copy(a, j) for j in range(per_dev)] for a in range(2)]
+
+    def terms(a, j):
+        for lo, size in tiles_of(width):
+            if a == 0:
+                v = dot(hid[j], w_out[j, :, lo : lo + size], (1, 0))
+            else:
+                v = dot(dpre[j], w_in[j, lo : lo + size, :], (1, 1))
+            term[a, j, :, :, lo : lo + size] = v.astype(BF16).reshape(2, half_rows, size)
+        mates[a][j].start()
+
+    def rs_copy(a, i):
+        src, to = ((sums.at[a, dd // 2], first), (sums.at[a, first // 2], first), (relay.at[a], second))[i]
+        return remote(src, landed.at[a, i], rs_s.at[a, i], rs_r.at[a, i], z, to)
+
+    rs = [[rs_copy(a, i) for i in range(3)] for a in range(2)]
+
+    def rs_start(a):
+        for j in range(per_dev):
+            mates[a][j].wait()
+
+        def column(n, carry):
+            at = pl.ds(pl.multiple_of(n * 128, 128), 128)
+            parts = [
+                term[a, j, core, :, at].astype(F32) + mate[a, j, :, at].astype(F32)
+                for j in range(per_dev)
+            ]
+            for chip in range(4):
+                picked = jnp.concatenate([p[chip * cap : (chip + 1) * cap] for p in parts], axis=0)
+                sums[a, chip, :, at] = picked.astype(BF16)
+            return carry
+
+        lax.fori_loop(0, width // 128, column, 0)
+        rs[a][0].start()
+        rs[a][1].start()
+
+    def rs_relay(a):
+        rs[a][0].wait()
+        relay[a] = (sums[a, second // 2].astype(F32) + landed[a, 0].astype(F32)).astype(BF16)
+        rs[a][2].start()
+
+    def back_copy(a, step):
+        to = (z + step) % zs
+        return remote(
+            zsend.at[a, to], zback.at[a, z], back_s.at[a, step - 1], back_r.at[a, step - 1], to, d
+        )
+
+    back = [[back_copy(a, step) for step in range(1, zs)] for a in range(2)]
+
+    def rs_end(a):
+        rs[a][1].wait()
+        rs[a][2].wait()
+        total = sums[a, d // 2].astype(F32) + landed[a, 1].astype(F32) + landed[a, 2].astype(F32)
+        for i in range(zs):
+            zsend[a, i] = total[:, i * cols : (i + 1) * cols].astype(BF16)
+        zback[a, pl.ds(z, 1)] = zsend[a, pl.ds(z, 1)]
+        for copy in back[a]:
+            copy.start()
+
+    def weight_grad_out(j):
+        def part(m, carry):
+            at = pl.ds(pl.multiple_of(m * 256, 256), 256)
+            left = hid[j, :, at]
+            for lo, size in tiles_of(width):
+                go[j, at, lo : lo + size] = dot(left, rows[1, j, :, lo : lo + size], (0, 0)).astype(BF16)
+            return carry
+
+        lax.fori_loop(0, hidden_here // 256, part, 0)
+        copy = pltpu.make_async_copy(go.at[j], go_hbm.at[j], osem.at[0, j])
+        copy.start()
+        return copy
+
+    def weight_grad_in(j):
+        def part(m, carry):
+            at = pl.ds(pl.multiple_of(m * 128, 128), 128)
+            gi[j, at, :] = dot(rows[0, j, :, at], dpre[j], (0, 0)).astype(BF16)
+            return carry
+
+        lax.fori_loop(0, width // 128, part, 0)
+        copy = pltpu.make_async_copy(gi.at[j], gi_hbm.at[j], osem.at[1, j])
+        copy.start()
+        return copy
+
+    gg = []
+    for step in range(1, zs):
+        gg.append(
+            remote(
+                gpart.at[z], gpart.at[z], gg_s.at[step - 1], gg_r.at[step - 1], (z + step) % zs, d
+            )
+        )
+
+    def combine(a):
+        for copy in back[a]:
+            copy.wait()
+        slot_rows = zback[a].reshape(zs * per_rows, cols)
+        views = [dot(place[k], slot_rows, (0, 0)) for k in range(2)]
+        if a == 1:
+            gtok_ref[...] = (views[0] + views[1]).astype(BF16)
+            return
+        out_ref[...] = (views[0] * gates_ref[:, 0:1] + views[1] * gates_ref[:, 1:2]).astype(BF16)
+        cot = cot_ref[...].astype(F32)
+        inner = [jnp.sum(cot * v, axis=1, keepdims=True) for v in views]
+        lane = lax.broadcasted_iota(jnp.int32, (tok_dev, 128), 1)
+        gpart[pl.ds(z, 1)] = jnp.where(lane == 0, inner[0], inner[1])[None]
+        for copy in gg:
+            copy.start()
+
+    assemble(0)
+    assemble(1)
+    forward(0)
+    forward_last(0)
+    for copy in w_copies:
+        copy.wait()
+    finish(0)
+    activation(0)
+    forward(1)
+    activation(1)
+    forward_last(1)
+    terms(0, 0)
+    terms(0, 1)
+    finish(1)
+    backward(0)
+    rs_start(0)
+    terms(1, 0)
+    backward(1)
+    rs_relay(0)
+    terms(1, 1)
+    rs_end(0)
+    outs = [weight_grad_out(0)]
+    rs_start(1)
+    outs.append(weight_grad_out(1))
+    rs_relay(1)
+    outs.append(weight_grad_in(0))
+    combine(0)
+    rs_end(1)
+    outs.append(weight_grad_in(1))
+    for copy in gg:
+        copy.wait()
+    total = gpart[0] + gpart[1] + gpart[2] + gpart[3]
+    gg_ref[...] = total[:, 0:2]
+    combine(1)
+    for a in range(2):
+        for copy in ag[a]:
+            copy.wait_send()
+    for copy in outs:
+        copy.wait()
+
+
+def fused_shards(tokens, routes, gate_values, expert_in, expert_out, cotangent):
+    tok_dev, cols = tokens.shape
+    zs = lax.axis_size("expert")
+    dps = lax.axis_size("dp")
+    per_dev, width, hidden_here = expert_in.shape
+    experts = per_dev * zs
+    cap = 5 * tok_dev // (2 * experts)
+    per_rows = per_dev * cap
+    all_rows = dps * cap
+    vmem = pl.BlockSpec(memory_space=pltpu.VMEM)
+    hbm = pl.BlockSpec(memory_space=pl.ANY)
+    dma = pltpu.SemaphoreType.DMA
+    return pl.pallas_call(
+        layer_kernel,
+        out_shape=(
+            jax.ShapeDtypeStruct(tokens.shape, BF16),
+            jax.ShapeDtypeStruct(tokens.shape, BF16),
+            jax.ShapeDtypeStruct(gate_values.shape, F32),
+            jax.ShapeDtypeStruct(expert_in.shape, BF16),
+            jax.ShapeDtypeStruct(expert_out.shape, BF16),
+        ),
+        in_specs=[vmem] * 5 + [hbm] * 2,
+        out_specs=(vmem, vmem, vmem, hbm, hbm),
+        scratch_shapes=[
+            pltpu.VMEM(expert_in.shape, BF16),
+            pltpu.VMEM(expert_out.shape, BF16),
+            pltpu.VMEM(expert_in.shape, BF16),
+            pltpu.VMEM(expert_out.shape, BF16),
+            pltpu.VMEM((2, zs, per_rows, cols), BF16),
+            pltpu.VMEM((2, zs, per_rows, cols), BF16),
+            pltpu.VMEM((2, dps, per_rows, width), BF16),
+            pltpu.VMEM((2, per_dev, all_rows, width), BF16),
+            pltpu.VMEM((per_dev, all_rows, hidden_here), BF16),
+            pltpu.VMEM((per_dev, all_rows, hidden_here), F32),
+            pltpu.VMEM((per_dev, all_rows, hidden_here), BF16),
+            pltpu.VMEM((2, per_dev, 2, all_rows // 2, width), BF16),
+            pltpu.VMEM((2, per_dev, all_rows // 2, width), BF16),
+            pltpu.VMEM((2, dps // 2, per_rows, width), BF16),
+            pltpu.VMEM((2, per_rows, width), BF16),
+            pltpu.VMEM((2, 3, per_rows, width), BF16),
+            pltpu.VMEM((2, zs, per_rows, cols), BF16),
+            pltpu.VMEM((2, zs, per_rows, cols), BF16),
+            pltpu.VMEM((2, experts * cap, tok_dev), BF16),
+            pltpu.VMEM((zs, tok_dev, 128), F32),
+            dma((2, per_dev)), dma((2, per_dev)),
+            dma((2, zs - 1)), dma((2, zs - 1)),
+            dma((2, 7)), dma((2, 7)),
+            dma((2, per_dev)), dma((2, per_dev)),
+            dma((2, 3)), dma((2, 3)),
+            dma((2, zs - 1)), dma((2, zs - 1)),
+            dma((zs - 1,)), dma((zs - 1,)),
+        ],
+        compiler_params=pltpu.CompilerParams(
+            collective_id=0, has_side_effects=True, vmem_limit_bytes=62 * 1024 * 1024
+        ),
+    )(tokens, cotangent, routes.T, gate_values.T, gate_values, expert_in, expert_out)
+
+
 def solution(mesh):
     placed = (
         P("dp", "expert"),
@@ -122,8 +493,9 @@
         P("expert", "dp", None),
         P("dp", "expert"),
     )
+    fused = mesh.shape["expert"] == 4 and mesh.shape["dp"] == 8
     return jax.shard_map(
-        shards,
+        fused_shards if fused else shards,
         mesh=mesh,
         in_specs=placed,
         out_specs=(

time: 207 us -> 90.6 us (0.44)
  waiting for transfers between devices: 101 us -> 0 us
  Pallas kernels: 0 us -> 73.4 us
  blocking collectives: 35.7 us -> 0 us
  matrix products: 30.9 us -> 0 us
  between operations: 14 us -> 0.64 us
  starting transfers between devices: 9.54 us -> 0 us
  local copies, waits for them, and re-layouts: 13.2 us -> 16.2 us
  other arithmetic: 2.09 us -> 0.01 us
    pallas_call x0 -> x1, Pallas kernels: none -> 73.4 us  [fused_shards(): pl.pallas_call(layer_kernel, out_shape=(jax.ShapeDtypeStruct(tokens.shape...]
    reduce_scatter x2 -> x0, waiting for transfers between devices: 57.4 us -> none  [shards(): lax.psum_scatter(term.reshape(lax.axis_size('dp') * slot_rows, full_width...]
    all_gather x2 -> x0, waiting for transfers between devices: 36.7 us -> none  [the longest x1 24 us: shards(): lax.all_gather(dy_moved.reshape(slot_rows, full_width), 'dp', axis=0, til...]
    dot_general x10 -> x0, matrix products: 30.9 us -> none  [the longest x1 7.18 us: shards(): jnp.einsum('bjcf,bjcd->jfd', hidden, dy_rows, preferred_element_type=jnp....]
    all_to_all x2 -> x0, blocking collectives: 25.3 us -> none  [the longest x1 14.7 us: shards(): lax.all_to_all(to_slots(pair_tokens), 'expert', split_axis=1, concat_axis...]
    psum x1 -> x0, blocking collectives: 10.4 us -> none  [shards(): grad_gates = lax.psum(gate_part, 'expert')]
    all_to_all x2 -> x0, starting transfers between devices: 9.19 us -> none  [the longest x1 4.6 us: shards(): lax.all_to_all(out_sum.reshape(slot_rows, groups, columns), 'expert', spl...]
    unnamed x14 -> x9, local copies, waits for them, and re-layouts: 2.49 us -> 11.5 us
  transfers between devices with their start and end apart: 6 -> 0, of which waited for: 5 -> 0; matrix products, arithmetic and copies ran while one was open for 14% -> 0% of each run, Pallas kernels for 0% -> 0%
where the time goes in v1:
time: 90.6 us; the launch traced here: 90.3 us
  Pallas kernels  73.4 us (81%)
  local copies, waits for them, and re-layouts  16.2 us (18%)
    pallas_call x1, Pallas kernels, fused_shards(): pl.pallas_call(layer_kernel, out_shape=(jax.ShapeDtypeStruct(tokens.shape...  73.4 us
    unnamed x9, local copies, waits for them, and re-layouts  11.5 us
    pallas_call x3, local copies, waits for them, and re-layouts, fused_shards(): pl.pallas_call(layer_kernel, out_shape=(jax.ShapeDtypeStruct(tokens.shape...  4.78 us

profile of v1, /device:TPU:0, one launch (start us, length us, event | category | flops | bytes accessed | tf_op | source)
XLA Modules:
  0.0 90.3 jit_solution(13339311503883400853)
XLA Ops:
  0.6 1.4 %copy.13.gates_ref = f32[128,2]{1,0:T(8,128)} copy(f32[128,2]{0,1:T(2,128)} %param.8) | data formatting | bytes 2048 | tf_op args[2]
  2.0 1.6 %copy.11.tok_ref = bf16[128,352]{1,0:T(8,128)(2,1)} copy(bf16[128,352]{0,1:T(8,128)(2,1)} %param.6) | data formatting | bytes 180224 | tf_op args[0]
  3.7 1.6 %copy.12.cot_ref = bf16[128,352]{1,0:T(8,128)(2,1)} copy(bf16[128,352]{0,1:T(8,128)(2,1)} %param.11) | data formatting | bytes 180224 | tf_op args[5]
  5.3 73.4 %shard_map.101 = (bf16[128,352]{1,0:T(8,128)(2,1)}, bf16[128,352]{1,0:T(8,128)(2,1)}, f32[128,2]{1,0:T(8,128)}, bf16[2,1408,768]{2,1,0:T(8,128)(2,1)}, bf16[2,768,1408]{2,1,0:T(8,128)(2,1)}) custom-call(bf16[128,352]{1,0:T(8,128)(2,1)} %copy.11.tok_ref, bf16[128,352]{1,0:T(8,128)(2,1)} %copy.12.cot_ref, s32[2,128]{1,0:T(2,128)} %bitcast.5, ...), custom_call_target="tpu_custom_call" | custom-call | tf_op jit(solution)/shard_map/pallas_call | solution.py:441
  78.7 1.6 %copy.14 = bf16[128,352]{0,1:T(8,128)(2,1)} copy(bf16[128,352]{1,0:T(8,128)(2,1)} %get-tuple-element.5) | data formatting | bytes 180224 | tf_op jit(solution)/shard_map/pallas_call | solution.py:441
  80.4 1.5 %copy.16 = f32[128,2]{0,1:T(2,128)} copy(f32[128,2]{1,0:T(8,128)} %get-tuple-element.7) | data formatting | bytes 2048 | tf_op jit(solution)/shard_map/pallas_call | solution.py:441
  81.8 0.0 slice-start
  81.8 1.7 %copy.15 = bf16[128,352]{0,1:T(8,128)(2,1)} copy(bf16[128,352]{1,0:T(8,128)(2,1)} %get-tuple-element.6) | data formatting | bytes 180224 | tf_op jit(solution)/shard_map/pallas_call | solution.py:441
  83.5 0.0 slice-start.1
  83.5 4.7 %copy.19 = bf16[2,1408,768]{2,1,0:T(8,128)(2,1)} copy(bf16[2,1408,768]{2,1,0:T(8,128)(2,1)} %get-tuple-element.18) | data formatting | bytes 8650752
  88.2 0.0 slice-done
  88.2 0.0 slice-done.1
  88.2 2.1 %copy.20 = bf16[2,768,1408]{2,1,0:T(8,128)(2,1)} copy(bf16[2,768,1408]{2,1,0:T(8,128)(2,1)S(1)} %bitcast.3) | data formatting | bytes 8650752
  (1 shorter events, 0.0 us)
Async XLA Ops:
  81.8 6.4 %slice-start = ((s8[4325376]{0:T(1024)(128)(4,1)}), s8[131072]{0:T(1024)(128)(4,1)S(1)}, s32[]{:S(2)}) async-start(s8[4325376]{0:T(1024)(128)(4,1)} %bitcast.2), calls=%async_computation | async-start | bytes 262144
  83.5 4.7 %slice-start.1 = ((s8[4325376]{0:T(1024)(128)(4,1)}), s8[4194304]{0:T(1024)(128)(4,1)S(1)}, s32[]{:S(2)}) async-start(s8[4325376]{0:T(1024)(128)(4,1)} %bitcast.2), calls=%async_computation.1 | async-start | bytes 8388608

commit v2 on v1

--- a/solution.py
+++ b/solution.py
@@ -129,13 +129,13 @@
 
 
 def layer_kernel(
-    tok_ref, cot_ref, routes_t, gates_t, gates_ref, w_in_hbm, w_out_hbm,
-    out_ref, gtok_ref, gg_ref, gi_hbm, go_hbm,
-    w_in, w_out, gi, go, slots, zgot, gath, rows, hid, slope, dpre,
+    tok_ref, cot_ref, routes_t, gates_t, w_in_hbm, w_out_hbm,
+    out_ref, gtok_ref, gg_ref, gi, go,
+    w_in, w_out, slots, zgot, gath, rows, hid, slope, dpre,
     term, mate, sums, relay, landed, zsend, zback, place, gpart,
-    wsem, osem, a2a_s, a2a_r, ag_s, ag_r, mate_s, mate_r, rs_s, rs_r, back_s, back_r, gg_s, gg_r,
+    wsem, a2a_s, a2a_r, ag_s, ag_r, mate_s, mate_r, rs_s, rs_r, back_s, back_r, gg_s, gg_r,
 ):
-    tok_dev, cols = tok_ref.shape
+    cols, tok_dev = tok_ref.shape
     zs = slots.shape[1]
     per_rows = slots.shape[2]
     per_dev = w_in.shape[0]
@@ -188,8 +188,8 @@
         place[k] = taken.astype(BF16)
         gate_col = gate_col + jnp.sum(taken * gates_t[k : k + 1, :], axis=1, keepdims=True)
     both = place[0] + place[1]
-    slots[0] = dot(both, tok_ref[...], (1, 0)).astype(BF16).reshape(zs, per_rows, cols)
-    slots[1] = (dot(both, cot_ref[...], (1, 0)) * gate_col).astype(BF16).reshape(zs, per_rows, cols)
+    slots[0] = dot(both, tok_ref[...], (1, 1)).astype(BF16).reshape(zs, per_rows, cols)
+    slots[1] = (dot(both, cot_ref[...], (1, 1)) * gate_col).astype(BF16).reshape(zs, per_rows, cols)
     for a in range(2):
         zgot[a, pl.ds(z, 1)] = slots[a, pl.ds(z, 1)]
 
@@ -346,9 +346,6 @@
             return carry
 
         lax.fori_loop(0, hidden_here // 256, part, 0)
-        copy = pltpu.make_async_copy(go.at[j], go_hbm.at[j], osem.at[0, j])
-        copy.start()
-        return copy
 
     def weight_grad_in(j):
         def part(m, carry):
@@ -357,9 +354,6 @@
             return carry
 
         lax.fori_loop(0, width // 128, part, 0)
-        copy = pltpu.make_async_copy(gi.at[j], gi_hbm.at[j], osem.at[1, j])
-        copy.start()
-        return copy
 
     gg = []
     for step in range(1, zs):
@@ -373,15 +367,15 @@
         for copy in back[a]:
             copy.wait()
         slot_rows = zback[a].reshape(zs * per_rows, cols)
-        views = [dot(place[k], slot_rows, (0, 0)) for k in range(2)]
+        views = [dot(slot_rows, place[k], (0, 0)) for k in range(2)]
         if a == 1:
             gtok_ref[...] = (views[0] + views[1]).astype(BF16)
             return
-        out_ref[...] = (views[0] * gates_ref[:, 0:1] + views[1] * gates_ref[:, 1:2]).astype(BF16)
+        out_ref[...] = (views[0] * gates_t[0:1, :] + views[1] * gates_t[1:2, :]).astype(BF16)
         cot = cot_ref[...].astype(F32)
-        inner = [jnp.sum(cot * v, axis=1, keepdims=True) for v in views]
-        lane = lax.broadcasted_iota(jnp.int32, (tok_dev, 128), 1)
-        gpart[pl.ds(z, 1)] = jnp.where(lane == 0, inner[0], inner[1])[None]
+        inner = [jnp.sum(cot * v, axis=0, keepdims=True) for v in views]
+        row = lax.broadcasted_iota(jnp.int32, (8, tok_dev), 0)
+        gpart[pl.ds(z, 1)] = jnp.where(row == 0, inner[0], inner[1])[None]
         for copy in gg:
             copy.start()
 
@@ -406,24 +400,22 @@
     rs_relay(0)
     terms(1, 1)
     rs_end(0)
-    outs = [weight_grad_out(0)]
+    weight_grad_out(0)
     rs_start(1)
-    outs.append(weight_grad_out(1))
+    weight_grad_out(1)
     rs_relay(1)
-    outs.append(weight_grad_in(0))
+    weight_grad_in(0)
     combine(0)
     rs_end(1)
-    outs.append(weight_grad_in(1))
+    weight_grad_in(1)
     for copy in gg:
         copy.wait()
     total = gpart[0] + gpart[1] + gpart[2] + gpart[3]
-    gg_ref[...] = total[:, 0:2]
+    gg_ref[...] = total[0:2]
     combine(1)
     for a in range(2):
         for copy in ag[a]:
             copy.wait_send()
-    for copy in outs:
-        copy.wait()
 
 
 def fused_shards(tokens, routes, gate_values, expert_in, expert_out, cotangent):
@@ -438,20 +430,18 @@
     vmem = pl.BlockSpec(memory_space=pltpu.VMEM)
     hbm = pl.BlockSpec(memory_space=pl.ANY)
     dma = pltpu.SemaphoreType.DMA
-    return pl.pallas_call(
+    layer_t, gtok_t, gates_grad_t, grad_in, grad_out = pl.pallas_call(
         layer_kernel,
         out_shape=(
-            jax.ShapeDtypeStruct(tokens.shape, BF16),
-            jax.ShapeDtypeStruct(tokens.shape, BF16),
-            jax.ShapeDtypeStruct(gate_values.shape, F32),
-            jax.ShapeDtypeStruct(expert_in.shape, BF16),
-            jax.ShapeDtypeStruct(expert_out.shape, BF16),
-        ),
-        in_specs=[vmem] * 5 + [hbm] * 2,
-        out_specs=(vmem, vmem, vmem, hbm, hbm),
-        scratch_shapes=[
+            pltpu.VMEM((cols, tok_dev), BF16),
+            pltpu.VMEM((cols, tok_dev), BF16),
+            pltpu.VMEM((2, tok_dev), F32),
             pltpu.VMEM(expert_in.shape, BF16),
             pltpu.VMEM(expert_out.shape, BF16),
+        ),
+        in_specs=[vmem] * 4 + [hbm] * 2,
+        out_specs=(vmem,) * 5,
+        scratch_shapes=[
             pltpu.VMEM(expert_in.shape, BF16),
             pltpu.VMEM(expert_out.shape, BF16),
             pltpu.VMEM((2, zs, per_rows, cols), BF16),
@@ -469,8 +459,8 @@
             pltpu.VMEM((2, zs, per_rows, cols), BF16),
             pltpu.VMEM((2, zs, per_rows, cols), BF16),
             pltpu.VMEM((2, experts * cap, tok_dev), BF16),
-            pltpu.VMEM((zs, tok_dev, 128), F32),
-            dma((2, per_dev)), dma((2, per_dev)),
+            pltpu.VMEM((zs, 8, tok_dev), F32),
+            dma((2, per_dev)),
             dma((2, zs - 1)), dma((2, zs - 1)),
             dma((2, 7)), dma((2, 7)),
             dma((2, per_dev)), dma((2, per_dev)),
@@ -479,9 +469,10 @@
             dma((zs - 1,)), dma((zs - 1,)),
         ],
         compiler_params=pltpu.CompilerParams(
-            collective_id=0, has_side_effects=True, vmem_limit_bytes=62 * 1024 * 1024
+            collective_id=0, has_side_effects=True, vmem_limit_bytes=46 * 1024 * 1024
         ),
-    )(tokens, cotangent, routes.T, gate_values.T, gate_values, expert_in, expert_out)
+    )(tokens.T, cotangent.T, routes.T, gate_values.T, expert_in, expert_out)
+    return (layer_t.T, gtok_t.T, gates_grad_t.T, grad_in, grad_out)
 
 
 def solution(mesh):

time: 90.6 us -> 75.9 us (0.84)
  local copies, waits for them, and re-layouts: 16.2 us -> 5.95 us
  Pallas kernels: 73.4 us -> 69.1 us
    unnamed x9 -> x5, local copies, waits for them, and re-layouts: 11.5 us -> 5.95 us
    pallas_call x3 -> x0, local copies, waits for them, and re-layouts: 4.78 us -> none  [fused_shards(): pl.pallas_call(layer_kernel, out_shape=(jax.ShapeDtypeStruct(tokens.shape...]
    pallas_call x1, Pallas kernels: 73.4 us -> 69.1 us  [fused_shards(): pl.pallas_call(layer_kernel, out_shape=(pltpu.VMEM((cols, tok_dev), BF16)...]
where the time goes in v2:
time: 75.9 us; the launch traced here: 75.7 us
  Pallas kernels  69.1 us (91%)
  local copies, waits for them, and re-layouts  5.95 us (8%)
    pallas_call x1, Pallas kernels, fused_shards(): pl.pallas_call(layer_kernel, out_shape=(pltpu.VMEM((cols, tok_dev), BF16)...  69.1 us
    unnamed x5, local copies, waits for them, and re-layouts  5.95 us

profile of v2, /device:TPU:0, one launch (start us, length us, event | category | flops | bytes accessed | tf_op | source)
XLA Modules:
  0.0 75.7 jit_solution(18092470741486781558)
XLA Ops:
  0.6 69.1 %shard_map.101 = (bf16[352,128]{1,0:T(8,128)(2,1)S(1)}, bf16[352,128]{1,0:T(8,128)(2,1)S(1)}, f32[2,128]{1,0:T(2,128)S(1)}, bf16[2,1408,768]{2,1,0:T(8,128)(2,1)S(1)}, bf16[2,768,1408]{2,1,0:T(8,128)(2,1)S(1)}) custom-call(bf16[352,128]{1,0:T(8,128)(2,1)} %bitcast.10, bf16[352,128]{1,0:T(8,128)(2,1)} %bitcast.11, s32[2,128]{1,0:T(2,128)} %bitcast.12, ...), custom_call_target="tpu_custom_call" | custom-call | tf_op jit(solution)/shard_map/pallas_call | solution.py:433
  69.8 0.6 copy.16
  70.4 0.6 copy.17
  71.1 0.6 copy.18
  71.6 2.1 %copy.19 = bf16[2,1408,768]{2,1,0:T(8,128)(2,1)} copy(bf16[2,1408,768]{2,1,0:T(8,128)(2,1)S(1)} %get-tuple-element.18) | data formatting | bytes 8650752
  73.7 2.1 %copy.20 = bf16[2,768,1408]{2,1,0:T(8,128)(2,1)} copy(bf16[2,768,1408]{2,1,0:T(8,128)(2,1)S(1)} %get-tuple-element.19) | data formatting | bytes 8650752

commit v3 on v2

--- a/solution.py
+++ b/solution.py
@@ -136,10 +136,7 @@
     wsem, a2a_s, a2a_r, ag_s, ag_r, mate_s, mate_r, rs_s, rs_r, back_s, back_r, gg_s, gg_r,
 ):
     cols, tok_dev = tok_ref.shape
-    zs = slots.shape[1]
-    per_rows = slots.shape[2]
-    per_dev = w_in.shape[0]
-    cap = per_rows // per_dev
+    zs, per_dev, cap = slots.shape[1:4]
     width, hidden_here = w_in.shape[1:]
     experts = zs * per_dev
     z = lax.axis_index("expert")
@@ -188,62 +185,71 @@
         place[k] = taken.astype(BF16)
         gate_col = gate_col + jnp.sum(taken * gates_t[k : k + 1, :], axis=1, keepdims=True)
     both = place[0] + place[1]
-    slots[0] = dot(both, tok_ref[...], (1, 1)).astype(BF16).reshape(zs, per_rows, cols)
-    slots[1] = (dot(both, cot_ref[...], (1, 1)) * gate_col).astype(BF16).reshape(zs, per_rows, cols)
-    for a in range(2):
-        zgot[a, pl.ds(z, 1)] = slots[a, pl.ds(z, 1)]
-
+    by_slot = (zs, per_dev, cap, cols)
+    a2a = [
+        [
+            [
+                remote(
+                    slots.at[a, (z + step) % zs, j], zgot.at[a, z, j],
+                    a2a_s.at[a, j, step - 1], a2a_r.at[a, j, step - 1], (z + step) % zs, d,
+                )
+                for step in range(1, zs)
+            ]
+            for j in range(per_dev)
+        ]
+        for a in range(2)
+    ]
+
+    def exchange(a, j):
+        for copy in a2a[a][j]:
+            copy.start()
+
+    slots[0] = dot(both, tok_ref[...], (1, 1)).reshape(by_slot).astype(BF16)
     pl.semaphore_wait(barrier, zs + 2)
-
-    a2a = []
-    for a in range(2):
-        a2a.append([])
-        for step in range(1, zs):
-            to = (z + step) % zs
-            copy = remote(
-                slots.at[a, to], zgot.at[a, z], a2a_s.at[a, step - 1], a2a_r.at[a, step - 1], to, d
-            )
-            copy.start()
-            a2a[a].append(copy)
-
-    def ag_copy(a, i):
+    exchange(0, 0)
+    exchange(0, 1)
+    zgot[0, pl.ds(z, 1)] = slots[0, pl.ds(z, 1)]
+    slots[1] = (dot(both, cot_ref[...], (1, 1)) * gate_col).reshape(by_slot).astype(BF16)
+    zgot[1, pl.ds(z, 1)] = slots[1, pl.ds(z, 1)]
+
+    def ag_copy(a, j, i):
         block, to = (
             (d, xn), (d, yn), (d, mate_d),
             (second, first), (xn, mate_d), (yn, mate_d), (dd, mate_d),
         )[i]
-        return remote(gath.at[a, block], gath.at[a, block], ag_s.at[a, i], ag_r.at[a, i], z, to)
-
-    ag = [[ag_copy(a, i) for i in range(7)] for a in range(2)]
-
-    def assemble(a):
-        for copy in a2a[a]:
+        here = gath.at[a, j, block]
+        return remote(here, here, ag_s.at[a, j, i], ag_r.at[a, j, i], z, to)
+
+    ag = [[[ag_copy(a, j, i) for i in range(7)] for j in range(per_dev)] for a in range(2)]
+
+    def arrive(a, j):
+        for copy in a2a[a][j]:
             copy.wait()
-        whole = jnp.concatenate([zgot[a, i].astype(F32) for i in range(zs)], axis=-1)
-        gath[a, pl.ds(d, 1)] = whole.astype(BF16)[None]
+
+    def assemble(a, j):
+        whole = jnp.concatenate([zgot[a, i, j].astype(F32) for i in range(zs)], axis=-1)
+        gath[a, j, pl.ds(d, 1)] = whole.astype(BF16)[None]
         for i in range(3):
-            ag[a][i].start()
-
-    def forward(a):
-        ag[a][0].wait_recv()
-        ag[a][1].wait_recv()
+            ag[a][j][i].start()
+
+    def forward(a, j):
+        ag[a][j][0].wait_recv()
+        ag[a][j][1].wait_recv()
         for i in (3, 4, 5):
-            ag[a][i].start()
-
-    def forward_last(a):
-        ag[a][3].wait_recv()
-        ag[a][6].start()
-
-    def finish(a):
+            ag[a][j][i].start()
+
+    def forward_last(a, j):
+        ag[a][j][3].wait_recv()
+        ag[a][j][6].start()
+
+    def finish(a, j):
         for i in (2, 4, 5, 6):
-            ag[a][i].wait_recv()
+            ag[a][j][i].wait_recv()
 
         def column(n, carry):
             at = pl.ds(pl.multiple_of(n * 128, 128), 128)
-            for half in range(2):
-                blocks = [gath[a, 2 * chip + half, :, at].astype(F32) for chip in range(4)]
-                for w in range(per_dev):
-                    picked = jnp.concatenate([b[w * cap : (w + 1) * cap] for b in blocks], axis=0)
-                    rows[a, w, half * 4 * cap : (half + 1) * 4 * cap, at] = picked.astype(BF16)
+            blocks = [gath[a, j, 2 * chip + half, :, at].astype(F32) for half in range(2) for chip in range(4)]
+            rows[a, j, :, at] = jnp.concatenate(blocks, axis=0).astype(BF16)
             return carry
 
         lax.fori_loop(0, width // 128, column, 0)
@@ -271,8 +277,6 @@
 
         lax.fori_loop(0, hidden_here // 256, column, 0)
 
-    half_rows = 4 * cap
-
     def mate_copy(a, j):
         return remote(
             term.at[a, j, 1 - core], mate.at[a, j], mate_s.at[a, j], mate_r.at[a, j], z, mate_d
@@ -286,56 +290,55 @@
                 v = dot(hid[j], w_out[j, :, lo : lo + size], (1, 0))
             else:
                 v = dot(dpre[j], w_in[j, lo : lo + size, :], (1, 1))
-            term[a, j, :, :, lo : lo + size] = v.astype(BF16).reshape(2, half_rows, size)
+            term[a, j, :, :, :, lo : lo + size] = v.reshape(2, 4, cap, size).astype(BF16)
         mates[a][j].start()
 
-    def rs_copy(a, i):
-        src, to = ((sums.at[a, dd // 2], first), (sums.at[a, first // 2], first), (relay.at[a], second))[i]
-        return remote(src, landed.at[a, i], rs_s.at[a, i], rs_r.at[a, i], z, to)
-
-    rs = [[rs_copy(a, i) for i in range(3)] for a in range(2)]
-
-    def rs_start(a):
-        for j in range(per_dev):
-            mates[a][j].wait()
+    def rs_copy(a, j, i):
+        src, to = (
+            (sums.at[a, j, dd // 2], first), (sums.at[a, j, first // 2], first), (relay.at[a, j], second)
+        )[i]
+        return remote(src, landed.at[a, j, i], rs_s.at[a, j, i], rs_r.at[a, j, i], z, to)
+
+    rs = [[[rs_copy(a, j, i) for i in range(3)] for j in range(per_dev)] for a in range(2)]
+
+    def rs_start(a, j):
+        mates[a][j].wait()
 
         def column(n, carry):
             at = pl.ds(pl.multiple_of(n * 128, 128), 128)
-            parts = [
-                term[a, j, core, :, at].astype(F32) + mate[a, j, :, at].astype(F32)
-                for j in range(per_dev)
-            ]
-            for chip in range(4):
-                picked = jnp.concatenate([p[chip * cap : (chip + 1) * cap] for p in parts], axis=0)
-                sums[a, chip, :, at] = picked.astype(BF16)
+            both_cores = term[a, j, core, :, :, at].astype(F32) + mate[a, j, :, :, at].astype(F32)
+            sums[a, j, :, :, at] = both_cores.astype(BF16)
             return carry
 
         lax.fori_loop(0, width // 128, column, 0)
-        rs[a][0].start()
-        rs[a][1].start()
-
-    def rs_relay(a):
-        rs[a][0].wait()
-        relay[a] = (sums[a, second // 2].astype(F32) + landed[a, 0].astype(F32)).astype(BF16)
-        rs[a][2].start()
-
-    def back_copy(a, step):
+        rs[a][j][0].start()
+        rs[a][j][1].start()
+
+    def rs_relay(a, j):
+        rs[a][j][0].wait()
+        relay[a, j] = (sums[a, j, second // 2].astype(F32) + landed[a, j, 0].astype(F32)).astype(BF16)
+        rs[a][j][2].start()
+
+    def back_copy(a, j, step):
         to = (z + step) % zs
         return remote(
-            zsend.at[a, to], zback.at[a, z], back_s.at[a, step - 1], back_r.at[a, step - 1], to, d
+            zsend.at[a, to, j], zback.at[a, z, j],
+            back_s.at[a, j, step - 1], back_r.at[a, j, step - 1], to, d,
         )
 
-    back = [[back_copy(a, step) for step in range(1, zs)] for a in range(2)]
-
-    def rs_end(a):
-        rs[a][1].wait()
-        rs[a][2].wait()
-        total = sums[a, d // 2].astype(F32) + landed[a, 1].astype(F32) + landed[a, 2].astype(F32)
+    back = [
+        [[back_copy(a, j, step) for step in range(1, zs)] for j in range(per_dev)] for a in range(2)
+    ]
+
+    def rs_end(a, j):
+        rs[a][j][1].wait()
+        rs[a][j][2].wait()
+        total = sums[a, j, d // 2].astype(F32) + landed[a, j, 1].astype(F32) + landed[a, j, 2].astype(F32)
         for i in range(zs):
-            zsend[a, i] = total[:, i * cols : (i + 1) * cols].astype(BF16)
-        zback[a, pl.ds(z, 1)] = zsend[a, pl.ds(z, 1)]
-        for copy in back[a]:
+            zsend[a, i, j] = total[:, i * cols : (i + 1) * cols].astype(BF16)
+        for copy in back[a][j]:
             copy.start()
+        zback[a, pl.ds(z, 1), j] = zsend[a, pl.ds(z, 1), j]
 
     def weight_grad_out(j):
         def part(m, carry):
@@ -364,9 +367,10 @@
         )
 
     def combine(a):
-        for copy in back[a]:
-            copy.wait()
-        slot_rows = zback[a].reshape(zs * per_rows, cols)
+        for j in range(per_dev):
+            for copy in back[a][j]:
+                copy.wait()
+        slot_rows = zback[a].astype(F32).reshape(experts * cap, cols).astype(BF16)
         views = [dot(slot_rows, place[k], (0, 0)) for k in range(2)]
         if a == 1:
             gtok_ref[...] = (views[0] + views[1]).astype(BF16)
@@ -379,34 +383,54 @@
         for copy in gg:
             copy.start()
 
-    assemble(0)
-    assemble(1)
-    forward(0)
-    forward_last(0)
+    arrive(0, 0)
+    assemble(0, 0)
+    arrive(0, 1)
+    exchange(1, 0)
+    exchange(1, 1)
+    assemble(0, 1)
+    forward(0, 0)
+    arrive(1, 0)
+    assemble(1, 0)
+    forward(0, 1)
+    forward_last(0, 0)
+    arrive(1, 1)
+    assemble(1, 1)
     for copy in w_copies:
         copy.wait()
-    finish(0)
+    finish(0, 0)
+    forward_last(0, 1)
     activation(0)
-    forward(1)
+    forward(1, 0)
+    terms(0, 0)
+    forward_last(1, 0)
+    forward(1, 1)
+    finish(0, 1)
     activation(1)
-    forward_last(1)
-    terms(0, 0)
+    rs_start(0, 0)
+    forward_last(1, 1)
     terms(0, 1)
-    finish(1)
+    finish(1, 0)
     backward(0)
-    rs_start(0)
+    rs_start(0, 1)
     terms(1, 0)
+    rs_relay(0, 0)
+    finish(1, 1)
     backward(1)
-    rs_relay(0)
+    rs_start(1, 0)
+    rs_relay(0, 1)
     terms(1, 1)
-    rs_end(0)
+    rs_end(0, 0)
+    rs_relay(1, 0)
+    rs_end(0, 1)
     weight_grad_out(0)
-    rs_start(1)
+    rs_start(1, 1)
     weight_grad_out(1)
-    rs_relay(1)
+    rs_end(1, 0)
+    rs_relay(1, 1)
+    combine(0)
     weight_grad_in(0)
-    combine(0)
-    rs_end(1)
+    rs_end(1, 1)
     weight_grad_in(1)
     for copy in gg:
         copy.wait()
@@ -414,8 +438,9 @@
     gg_ref[...] = total[0:2]
     combine(1)
     for a in range(2):
-        for copy in ag[a]:
-            copy.wait_send()
+        for j in range(per_dev):
+            for copy in ag[a][j]:
+                copy.wait_send()
 
 
 def fused_shards(tokens, routes, gate_values, expert_in, expert_out, cotangent):
@@ -425,7 +450,6 @@
     per_dev, width, hidden_here = expert_in.shape
     experts = per_dev * zs
     cap = 5 * tok_dev // (2 * experts)
-    per_rows = per_dev * cap
     all_rows = dps * cap
     vmem = pl.BlockSpec(memory_space=pltpu.VMEM)
     hbm = pl.BlockSpec(memory_space=pl.ANY)
@@ -444,28 +468,28 @@
         scratch_shapes=[
             pltpu.VMEM(expert_in.shape, BF16),
             pltpu.VMEM(expert_out.shape, BF16),
-            pltpu.VMEM((2, zs, per_rows, cols), BF16),
-            pltpu.VMEM((2, zs, per_rows, cols), BF16),
-            pltpu.VMEM((2, dps, per_rows, width), BF16),
+            pltpu.VMEM((2, zs, per_dev, cap, cols), BF16),
+            pltpu.VMEM((2, zs, per_dev, cap, cols), BF16),
+            pltpu.VMEM((2, per_dev, dps, cap, width), BF16),
             pltpu.VMEM((2, per_dev, all_rows, width), BF16),
             pltpu.VMEM((per_dev, all_rows, hidden_here), BF16),
             pltpu.VMEM((per_dev, all_rows, hidden_here), F32),
             pltpu.VMEM((per_dev, all_rows, hidden_here), BF16),
-            pltpu.VMEM((2, per_dev, 2, all_rows // 2, width), BF16),
-            pltpu.VMEM((2, per_dev, all_rows // 2, width), BF16),
-            pltpu.VMEM((2, dps // 2, per_rows, width), BF16),
-            pltpu.VMEM((2, per_rows, width), BF16),
-            pltpu.VMEM((2, 3, per_rows, width), BF16),
-            pltpu.VMEM((2, zs, per_rows, cols), BF16),
-            pltpu.VMEM((2, zs, per_rows, cols), BF16),
+            pltpu.VMEM((2, per_dev, 2, dps // 2, cap, width), BF16),
+            pltpu.VMEM((2, per_dev, dps // 2, cap, width), BF16),
+            pltpu.VMEM((2, per_dev, dps // 2, cap, width), BF16),
+            pltpu.VMEM((2, per_dev, cap, width), BF16),
+            pltpu.VMEM((2, per_dev, 3, cap, width), BF16),
+            pltpu.VMEM((2, zs, per_dev, cap, cols), BF16),
+            pltpu.VMEM((2, zs, per_dev, cap, cols), BF16),
             pltpu.VMEM((2, experts * cap, tok_dev), BF16),
             pltpu.VMEM((zs, 8, tok_dev), F32),
             dma((2, per_dev)),
-            dma((2, zs - 1)), dma((2, zs - 1)),
-            dma((2, 7)), dma((2, 7)),
+            dma((2, per_dev, zs - 1)), dma((2, per_dev, zs - 1)),
+            dma((2, per_dev, 7)), dma((2, per_dev, 7)),
             dma((2, per_dev)), dma((2, per_dev)),
-            dma((2, 3)), dma((2, 3)),
-            dma((2, zs - 1)), dma((2, zs - 1)),
+            dma((2, per_dev, 3)), dma((2, per_dev, 3)),
+            dma((2, per_dev, zs - 1)), dma((2, per_dev, zs - 1)),
             dma((zs - 1,)), dma((zs - 1,)),
         ],
         compiler_params=pltpu.CompilerParams(

time: 75.9 us -> 67.5 us (0.89)
  Pallas kernels: 69.1 us -> 60.7 us
    pallas_call x1, Pallas kernels: 69.1 us -> 60.7 us  [fused_shards(): pl.pallas_call(layer_kernel, out_shape=(pltpu.VMEM((cols, tok_dev), BF16)...]
where the time goes in v3:
time: 67.5 us; the launch traced here: 67.3 us
  Pallas kernels  60.7 us (90%)
  local copies, waits for them, and re-layouts  5.95 us (9%)
    pallas_call x1, Pallas kernels, fused_shards(): pl.pallas_call(layer_kernel, out_shape=(pltpu.VMEM((cols, tok_dev), BF16)...  60.7 us
    unnamed x5, local copies, waits for them, and re-layouts  5.95 us

profile of v3, /device:TPU:0, one launch (start us, length us, event | category | flops | bytes accessed | tf_op | source)
XLA Modules:
  0.0 67.3 jit_solution(5509075195440191952)
XLA Ops:
  0.6 60.7 %shard_map.101 = (bf16[352,128]{1,0:T(8,128)(2,1)S(1)}, bf16[352,128]{1,0:T(8,128)(2,1)S(1)}, f32[2,128]{1,0:T(2,128)S(1)}, bf16[2,1408,768]{2,1,0:T(8,128)(2,1)S(1)}, bf16[2,768,1408]{2,1,0:T(8,128)(2,1)S(1)}) custom-call(bf16[352,128]{1,0:T(8,128)(2,1)} %bitcast.10, bf16[352,128]{1,0:T(8,128)(2,1)} %bitcast.11, s32[2,128]{1,0:T(2,128)} %bitcast.12, ...), custom_call_target="tpu_custom_call" | custom-call | tf_op jit(solution)/shard_map/pallas_call | solution.py:457
  61.4 0.6 copy.16
  62.0 0.6 copy.17
  62.6 0.6 copy.18
  63.2 2.1 %copy.19 = bf16[2,1408,768]{2,1,0:T(8,128)(2,1)} copy(bf16[2,1408,768]{2,1,0:T(8,128)(2,1)S(1)} %get-tuple-element.18) | data formatting | bytes 8650752
  65.3 2.1 %copy.20 = bf16[2,768,1408]{2,1,0:T(8,128)(2,1)} copy(bf16[2,768,1408]{2,1,0:T(8,128)(2,1)S(1)} %get-tuple-element.19) | data formatting | bytes 8650752
